TPU v7x, 32 devices: a whole 2x2x4 slice. The times are simulated.
32 devices in a mesh: rep: 2 (over y), fsdp: 4 (over z), seq: 4 (over x, core).
Axes of the slice: x: 2, y: 2, z: 4, core: 2. Of those that a mesh axis runs over, the one named last changes fastest.
Arguments:
- latents: bfloat16 [8, 1024, 1152], P(('rep', 'fsdp'), 'seq'), may hold values from -6 to 6
- cond: bfloat16 [8, 1152], P(('rep', 'fsdp')), may hold values from -6 to 6
- w_ada: bfloat16 [1152, 6912], P(('fsdp', 'seq')), may hold values from -0.25 to 0.25
- b_ada: bfloat16 [6912], P(('fsdp', 'seq')), may hold values from -3 to 3
- w_qkv: bfloat16 [1152, 3456], P(('fsdp', 'seq')), may hold values from -0.1875 to 0.1875
- b_qv: bfloat16 [2304], P(('fsdp', 'seq')), may hold values from -3 to 3
- w_out: bfloat16 [1152, 1152], P(('fsdp', 'seq')), may hold values from -1.5 to 1.5
- b_out: bfloat16 [1152], P(('fsdp', 'seq')), may hold values from -3 to 3
- w_one: bfloat16 [1152, 4608], P(('fsdp', 'seq')), may hold values from -0.1875 to 0.1875
- b_one: bfloat16 [4608], P(('fsdp', 'seq')), may hold values from -3 to 3
- w_two: bfloat16 [4608, 1152], P(('fsdp', 'seq')), may hold values from -0.09375 to 0.09375
- b_two: bfloat16 [1152], P(('fsdp', 'seq')), may hold values from -3 to 3
- cotangent: bfloat16 [8, 1024, 1152], P(('rep', 'fsdp'), 'seq'), may hold values from -6 to 6
Outputs:
- block_out: bfloat16 [8, 1024, 1152], P(('rep', 'fsdp'), 'seq')
- grad_latents: float32 [8, 1024, 1152], P(('rep', 'fsdp'), 'seq')
- grad_cond: float32 [8, 1152], P(('rep', 'fsdp'))
- grad_w_ada: float32 [1152, 6912], P(('fsdp', 'seq'))
- grad_b_ada: float32 [6912], P(('fsdp', 'seq'))
- grad_w_qkv: float32 [1152, 3456], P(('fsdp', 'seq'))
- grad_b_qv: float32 [2304], P(('fsdp', 'seq'))
- grad_w_out: float32 [1152, 1152], P(('fsdp', 'seq'))
- grad_b_out: float32 [1152], P(('fsdp', 'seq'))
- grad_w_one: float32 [1152, 4608], P(('fsdp', 'seq'))
- grad_b_one: float32 [4608], P(('fsdp', 'seq'))
- grad_w_two: float32 [4608, 1152], P(('fsdp', 'seq'))
- grad_b_two: float32 [1152], P(('fsdp', 'seq'))
All inputs are finite; a program needn't handle non-finite values.
Results may differ from a plain program's by a relative error of at most 0.014.
The roundings to bfloat16 on the way count: a program that leaves them out, or rounds other values in their place, can miss the bound.
Values may be sent and summed in bfloat16 or wider, within the bound.
A program may use at most 448 MiB of HBM per device.

v0:
```python
import math
import jax
import jax.numpy as jnp
from jax import lax
from jax.sharding import PartitionSpec as P

H = 16
epsilon = 1e-06
gelu_coef = math.sqrt(2.0 / math.pi)


def norm_stats(values):
    center = values - jnp.mean(values, axis=-1, keepdims=True)
    inv_std = lax.rsqrt(jnp.mean(center * center, axis=-1, keepdims=True) + epsilon)
    return (center * inv_std, inv_std)


def norm_back(grad, normed, inv_std):
    return inv_std * (
        grad
        - jnp.mean(grad, axis=-1, keepdims=True)
        - normed * jnp.mean(grad * normed, axis=-1, keepdims=True)
    )


def gelu_tanh(values):
    inner = gelu_coef * (values + 0.044715 * values * values * values)
    return 0.5 * values * (1.0 + jnp.tanh(inner))


def gelu_slope(values):
    inner = gelu_coef * (values + 0.044715 * values * values * values)
    tanh_val = jnp.tanh(inner)
    return 0.5 * (1.0 + tanh_val) + 0.5 * values * (1.0 - tanh_val * tanh_val) * gelu_coef * (
        1.0 + 3.0 * 0.044715 * values * values
    )


def row_dot(left, right):
    return jnp.dot(left, right, preferred_element_type=jnp.float32)


def back_dot(grad, weight):
    return lax.dot_general(
        grad, weight, (((1,), (1,)), ((), ())), preferred_element_type=jnp.float32
    )


def outer_dot(left, grad):
    return lax.dot_general(left, grad, (((0,), (0,)), ((), ())), preferred_element_type=jnp.float32)


def pack_rows(arrays, groups):
    return jnp.concatenate([array.reshape(groups, -1) for array in arrays], axis=1).reshape(-1)


def unpack_rows(flat, layouts, groups):
    pieces = []
    offset = 0
    for layout in layouts:
        amount = math.prod(layout) // groups
        piece = flat[offset : offset + amount].reshape((layout[0] // groups,) + tuple(layout[1:]))
        pieces.append(piece)
        offset = offset + amount
    return pieces


def split_blocks(array, block_len):
    shape = array.shape
    return jnp.moveaxis(
        array.reshape(shape[:2] + (shape[2] // block_len, block_len) + shape[3:]), 2, 0
    )


def join_blocks(array):
    moved = jnp.moveaxis(array, 0, 2)
    shape = moved.shape
    return moved.reshape(shape[:2] + (shape[2] * shape[3],) + shape[4:])


def attention_forward(queries, key_rows, val_rows):
    length = queries.shape[2]
    head_size = queries.shape[3]
    block_len = min(512, length)
    score_scale = head_size ** (-0.5)

    def one_block(query_block):
        scores = (
            jnp.einsum("bhqd,bhkd->bhqk", query_block, key_rows, preferred_element_type=jnp.float32)
            * score_scale
        )
        highest = jnp.max(scores, axis=-1, keepdims=True)
        raised = jnp.exp(scores - highest)
        summed = jnp.sum(raised, axis=-1, keepdims=True)
        probs_low = (raised / summed).astype(jnp.bfloat16)
        result = jnp.einsum(
            "bhqk,bhkd->bhqd", probs_low, val_rows, preferred_element_type=jnp.float32
        )
        return (result.astype(jnp.bfloat16), (highest + jnp.log(summed))[..., 0])

    outputs, log_totals = lax.map(one_block, split_blocks(queries, block_len))
    return (join_blocks(outputs), join_blocks(log_totals))


def attention_backward(queries, key_rows, val_rows, log_totals, grad_out):
    length = queries.shape[2]
    head_size = queries.shape[3]
    block_len = min(512, length)
    score_scale = head_size ** (-0.5)

    def one_block(carried, pieces):
        grad_keys, grad_vals = carried
        query_block, grad_block, lse_block = pieces
        scores = (
            jnp.einsum("bhqd,bhkd->bhqk", query_block, key_rows, preferred_element_type=jnp.float32)
            * score_scale
        )
        attn_probs = jnp.exp(scores - lse_block[..., None])
        grad_probs = jnp.einsum(
            "bhqd,bhkd->bhqk", grad_block, val_rows, preferred_element_type=jnp.float32
        )
        row_inner = jnp.sum(attn_probs * grad_probs, axis=-1, keepdims=True)
        grad_scores = (attn_probs * (grad_probs - row_inner)).astype(jnp.bfloat16)
        grad_query = (
            jnp.einsum("bhqk,bhkd->bhqd", grad_scores, key_rows, preferred_element_type=jnp.float32)
            * score_scale
        )
        grad_keys = (
            grad_keys
            + jnp.einsum(
                "bhqk,bhqd->bhkd", grad_scores, query_block, preferred_element_type=jnp.float32
            )
            * score_scale
        )
        grad_vals = grad_vals + jnp.einsum(
            "bhqk,bhqd->bhkd",
            attn_probs.astype(jnp.bfloat16),
            grad_block,
            preferred_element_type=jnp.float32,
        )
        return ((grad_keys, grad_vals), grad_query)

    zeros_start = jnp.zeros(key_rows.shape, jnp.float32)
    pieces = (
        split_blocks(queries, block_len),
        split_blocks(grad_out, block_len),
        split_blocks(log_totals, block_len),
    )
    (grad_keys, grad_vals), grad_queries = lax.scan(one_block, (zeros_start, zeros_start), pieces)
    return (join_blocks(grad_queries), grad_keys, grad_vals)


def on_device(
    latents, cond, w_ada, b_ada, w_qkv, b_qv, w_out, b_out, w_one, b_one, w_two, b_two, cotangent
):
    latent_count, local_len, width = latents.shape
    token_rows = latent_count * local_len
    head_count = H
    head_size = width // head_count
    seq_count = lax.axis_size("seq")
    group_size = lax.axis_size(("fsdp", "seq"))
    local_heads = head_count // seq_count
    full_len = local_len * seq_count
    owner = lax.axis_index(("fsdp", "seq"))
    own_rows = w_ada.shape[0]
    bias_cols = b_ada.shape[0]
    first_latent = lax.axis_index(("rep", "fsdp")) * latent_count
    cond_float = cond.astype(jnp.float32)
    cond_sigmoid = jax.nn.sigmoid(cond_float)
    silu_cond = (cond_float * cond_sigmoid).astype(jnp.bfloat16)
    silu_every = lax.all_gather(silu_cond, ("rep", "fsdp"), axis=0, tiled=True)
    silu_owned = lax.dynamic_slice_in_dim(silu_every, owner * own_rows, own_rows, 1)
    ada_part = row_dot(silu_owned, w_ada)
    bias_slot = (
        lax.dynamic_slice_in_dim(ada_part, owner * bias_cols, bias_cols, 1)
        + b_ada.astype(jnp.float32)[None, :]
    )
    ada_part = lax.dynamic_update_slice_in_dim(ada_part, bias_slot, owner * bias_cols, 1)
    modulation_every = lax.psum(ada_part, ("fsdp", "seq"))
    modulation = lax.dynamic_slice_in_dim(modulation_every, first_latent, latent_count, 0)
    shift_one, scale_one, gate_one, shift_two, scale_two, gate_two = jnp.split(
        modulation[:, None, :], 6, axis=2
    )
    full_fwd = (
        lax.all_gather(w_qkv, ("fsdp", "seq"), axis=0, tiled=True),
        lax.all_gather(b_qv, ("fsdp", "seq"), axis=0, tiled=True),
        lax.all_gather(w_out, ("fsdp", "seq"), axis=0, tiled=True),
        lax.all_gather(b_out, ("fsdp", "seq"), axis=0, tiled=True),
        lax.all_gather(w_one, ("fsdp", "seq"), axis=0, tiled=True),
        lax.all_gather(b_one, ("fsdp", "seq"), axis=0, tiled=True),
        lax.all_gather(w_two, ("fsdp", "seq"), axis=0, tiled=True),
        lax.all_gather(b_two, ("fsdp", "seq"), axis=0, tiled=True),
    )
    qkv_full, qv_bias, out_full, out_bias, one_full, one_bias, two_full, two_bias = full_fwd
    inputs = latents.astype(jnp.float32)
    normed_one, inv_one = norm_stats(inputs)
    mixed_one = (
        (normed_one * (1.0 + scale_one) + shift_one).astype(jnp.bfloat16).reshape(token_rows, width)
    )
    bias_full = jnp.concatenate(
        [qv_bias[:width], jnp.zeros((width,), jnp.bfloat16), qv_bias[width:]]
    ).astype(jnp.float32)
    projected = (row_dot(mixed_one, qkv_full) + bias_full).astype(jnp.bfloat16)
    token_heads = projected.reshape(latent_count, local_len, 3, head_count, head_size).transpose(
        2, 0, 3, 1, 4
    )
    token_heads = token_heads.reshape(3, latent_count, head_count, local_len * head_size)
    head_tokens = lax.all_to_all(token_heads, "seq", split_axis=2, concat_axis=3, tiled=True)
    head_tokens = head_tokens.reshape(3, latent_count, local_heads, full_len, head_size)
    queries = head_tokens[0]
    key_rows = head_tokens[1]
    val_rows = head_tokens[2]
    attended, log_totals = attention_forward(queries, key_rows, val_rows)
    back_tokens = lax.all_to_all(
        attended.reshape(latent_count, local_heads, full_len * head_size),
        "seq",
        split_axis=2,
        concat_axis=1,
        tiled=True,
    )
    merged = (
        back_tokens.reshape(latent_count, head_count, local_len, head_size)
        .transpose(0, 2, 1, 3)
        .reshape(token_rows, width)
    )
    branch_one = (row_dot(merged, out_full) + out_bias.astype(jnp.float32)).reshape(
        latent_count, local_len, width
    )
    residual = inputs + gate_one * branch_one
    normed_two, inv_two = norm_stats(residual)
    mixed_two = (
        (normed_two * (1.0 + scale_two) + shift_two).astype(jnp.bfloat16).reshape(token_rows, width)
    )
    hidden_pre = row_dot(mixed_two, one_full) + one_bias.astype(jnp.float32)
    hidden_act = gelu_tanh(hidden_pre).astype(jnp.bfloat16)
    branch_two = (row_dot(hidden_act, two_full) + two_bias.astype(jnp.float32)).reshape(
        latent_count, local_len, width
    )
    block_out = (residual + gate_two * branch_two).astype(jnp.bfloat16)
    full_back = (
        lax.all_gather(w_qkv, ("fsdp", "seq"), axis=0, tiled=True),
        lax.all_gather(b_qv, ("fsdp", "seq"), axis=0, tiled=True),
        lax.all_gather(w_out, ("fsdp", "seq"), axis=0, tiled=True),
        lax.all_gather(b_out, ("fsdp", "seq"), axis=0, tiled=True),
        lax.all_gather(w_one, ("fsdp", "seq"), axis=0, tiled=True),
        lax.all_gather(b_one, ("fsdp", "seq"), axis=0, tiled=True),
        lax.all_gather(w_two, ("fsdp", "seq"), axis=0, tiled=True),
        lax.all_gather(b_two, ("fsdp", "seq"), axis=0, tiled=True),
    )
    qkv_back = full_back[0]
    out_back = full_back[2]
    one_back = full_back[4]
    two_back = full_back[6]
    grad_out = cotangent.astype(jnp.float32)
    grad_two = (gate_two * grad_out).astype(jnp.bfloat16).reshape(token_rows, width)
    gate_two_grad = jnp.sum(grad_out * branch_two, axis=1)
    two_w_grad = outer_dot(hidden_act, grad_two)
    two_b_grad = jnp.sum(grad_two, axis=0, dtype=jnp.float32)
    grad_pre = (back_dot(grad_two, two_back) * gelu_slope(hidden_pre)).astype(jnp.bfloat16)
    one_w_grad = outer_dot(mixed_two, grad_pre)
    one_b_grad = jnp.sum(grad_pre, axis=0, dtype=jnp.float32)
    grad_mixed_two = back_dot(grad_pre, one_back).reshape(latent_count, local_len, width)
    shift_two_grad = jnp.sum(grad_mixed_two, axis=1)
    scale_two_grad = jnp.sum(grad_mixed_two * normed_two, axis=1)
    grad_resid = grad_out + norm_back(grad_mixed_two * (1.0 + scale_two), normed_two, inv_two)
    mlp_layouts = (one_w_grad.shape, one_b_grad.shape, two_w_grad.shape, two_b_grad.shape)
    mlp_flat = lax.psum_scatter(
        pack_rows((one_w_grad, one_b_grad, two_w_grad, two_b_grad), group_size),
        ("fsdp", "seq"),
        scatter_dimension=0,
        tiled=True,
    )
    grad_branch = (gate_one * grad_resid).astype(jnp.bfloat16).reshape(token_rows, width)
    gate_one_grad = jnp.sum(grad_resid * branch_one, axis=1)
    out_w_grad = outer_dot(merged, grad_branch)
    out_b_grad = jnp.sum(grad_branch, axis=0, dtype=jnp.float32)
    grad_merged = back_dot(grad_branch, out_back).astype(jnp.bfloat16)
    grad_heads = grad_merged.reshape(latent_count, local_len, head_count, head_size).transpose(
        0, 2, 1, 3
    )
    grad_heads = grad_heads.reshape(latent_count, head_count, local_len * head_size)
    grad_heads = lax.all_to_all(grad_heads, "seq", split_axis=1, concat_axis=2, tiled=True)
    grad_heads = grad_heads.reshape(latent_count, local_heads, full_len, head_size)
    grad_queries, grad_keys, grad_vals = attention_backward(
        queries, key_rows, val_rows, log_totals, grad_heads
    )
    stacked = jnp.stack([grad_queries, grad_keys, grad_vals]).astype(jnp.bfloat16)
    stacked = stacked.reshape(3, latent_count, local_heads, full_len * head_size)
    grad_tokens = lax.all_to_all(stacked, "seq", split_axis=3, concat_axis=2, tiled=True)
    grad_proj = grad_tokens.reshape(3, latent_count, head_count, local_len, head_size).transpose(
        1, 3, 0, 2, 4
    )
    grad_proj = grad_proj.reshape(token_rows, 3 * width)
    qkv_w_grad = outer_dot(mixed_one, grad_proj)
    proj_sums = jnp.sum(grad_proj, axis=0, dtype=jnp.float32)
    qv_b_grad = jnp.concatenate([proj_sums[:width], proj_sums[2 * width :]])
    grad_mixed_one = back_dot(grad_proj, qkv_back).reshape(latent_count, local_len, width)
    shift_one_grad = jnp.sum(grad_mixed_one, axis=1)
    scale_one_grad = jnp.sum(grad_mixed_one * normed_one, axis=1)
    grad_inputs = grad_resid + norm_back(grad_mixed_one * (1.0 + scale_one), normed_one, inv_one)
    partial_mod = jnp.concatenate(
        [
            shift_one_grad,
            scale_one_grad,
            gate_one_grad,
            shift_two_grad,
            scale_two_grad,
            gate_two_grad,
        ],
        axis=1,
    )
    mod_grad = lax.psum(partial_mod, "seq").astype(jnp.bfloat16)
    mod_every = lax.all_gather(mod_grad, ("rep", "fsdp"), axis=0, tiled=True)
    ada_w_grad = outer_dot(silu_owned, mod_every)
    ada_b_grad = jnp.sum(
        lax.dynamic_slice_in_dim(mod_every, owner * bias_cols, bias_cols, 1),
        axis=0,
        dtype=jnp.float32,
    )
    cond_part = back_dot(mod_every, w_ada)
    cond_every = lax.all_gather(cond_part, ("fsdp", "seq"), axis=1, tiled=True)
    cond_lin = lax.dynamic_slice_in_dim(cond_every, first_latent, latent_count, 0)
    cond_grad = cond_lin * cond_sigmoid * (1.0 + cond_float * (1.0 - cond_sigmoid))
    attn_layouts = (qkv_w_grad.shape, qv_b_grad.shape, out_w_grad.shape, out_b_grad.shape)
    attn_flat = lax.psum_scatter(
        pack_rows((qkv_w_grad, qv_b_grad, out_w_grad, out_b_grad), group_size),
        ("fsdp", "seq"),
        scatter_dimension=0,
        tiled=True,
    )
    attn_total, mlp_total = (
        lax.psum(attn_flat.astype(jnp.bfloat16), "rep").astype(jnp.float32),
        lax.psum(mlp_flat.astype(jnp.bfloat16), "rep").astype(jnp.float32),
    )
    attn_parts = unpack_rows(attn_total, attn_layouts, group_size)
    mlp_parts = unpack_rows(mlp_total, mlp_layouts, group_size)
    return (
        block_out,
        grad_inputs,
        cond_grad,
        ada_w_grad,
        ada_b_grad,
        attn_parts[0],
        attn_parts[1],
        attn_parts[2],
        attn_parts[3],
        mlp_parts[0],
        mlp_parts[1],
        mlp_parts[2],
        mlp_parts[3],
    )


def solution(mesh):
    in_specs = (
        P(("rep", "fsdp"), "seq", None),
        P(("rep", "fsdp"), None),
        P(("fsdp", "seq"), None),
        P(("fsdp", "seq")),
        P(("fsdp", "seq"), None),
        P(("fsdp", "seq")),
        P(("fsdp", "seq"), None),
        P(("fsdp", "seq")),
        P(("fsdp", "seq"), None),
        P(("fsdp", "seq")),
        P(("fsdp", "seq"), None),
        P(("fsdp", "seq")),
        P(("rep", "fsdp"), "seq", None),
    )
    out_specs = (
        P(("rep", "fsdp"), "seq", None),
        P(("rep", "fsdp"), "seq", None),
        P(("rep", "fsdp"), None),
        P(("fsdp", "seq"), None),
        P(("fsdp", "seq")),
        P(("fsdp", "seq"), None),
        P(("fsdp", "seq")),
        P(("fsdp", "seq"), None),
        P(("fsdp", "seq")),
        P(("fsdp", "seq"), None),
        P(("fsdp", "seq")),
        P(("fsdp", "seq"), None),
        P(("fsdp", "seq")),
    )
    return jax.shard_map(
        on_device, mesh=mesh, in_specs=in_specs, out_specs=out_specs, check_vma=False
    )
```

profile of v0, /device:TPU:0, one launch (start us, length us, event | category | flops | bytes accessed | tf_op | source)
XLA Modules:
  0.0 3231.1 jit_solution(2037017178745607638)
XLA Ops:
  8.7 32.3 %all-gather = bf16[8,1,1152]{2,1,0:T(2,128)(2,1)S(1)} all-gather(bf16[1,1,1152]{2,1,0:T(2,128)(2,1)S(1)} %get-tuple-element.247), channel_id=1, replica_groups=mesh['rep'=2,'fsdp'=4,'seq'=4] {'rep','fsdp'}, dimensions={0}, use_global_device_ids=true | all-gather | bytes 20736 | tf_op jit(solution)/shard_map/all_gather | solution.py:171
  50.0 57.8 %all-reduce.7 = (bf16[2304]{0:T(1024)(128)(2,1)S(1)}, bf16[1152]{0:T(1024)(128)(2,1)S(1)}, bf16[1152]{0:T(1024)(128)(2,1)S(1)}, bf16[4608]{0:T(1024)(128)(2,1)S(1)}) all-reduce(bf16[2304]{0:T(1024)(128)(2,1)S(1)} %dynamic-update-slice, bf16[1152]{0:T(1024)(128)(2,1)S(1)} %dynamic-update-slice.1, ...), channel_id=1, replica_groups=mesh['rep'=2,'fsdp'=4,'seq'=4] {'fsdp','seq'}, use_global_device_ids=true, to_apply=%add | all-reduce | flops 9216 | bytes 36864
  108.3 25.0 all-reduce.13.cloned.1.call-done
  134.9 73.7 %all-gather.8.cloned.1.call-done = bf16[1152,3456]{1,0:T(8,128)(2,1)} async-done(((bf16[72,3456]{1,0:T(8,128)(2,1)}), bf16[1152,3456]{1,0:T(8,128)(2,1)}) %all-gather.8.cloned.1.call-update) | async-done | bytes 7962640 | tf_op jit(solution)/shard_map/all_gather | solution.py:185
  208.7 7.2 fusion.46
  221.3 8.1 reshape.492
  233.5 35.5 %all-to-all-done = bf16[3,1,16,18432]{3,0,1,2:T(4,128)(2,1)S(1)} async-done(((bf16[3,1,16,18432]{3,0,1,2:T(4,128)(2,1)}), bf16[3,1,16,18432]{3,0,1,2:T(4,128)(2,1)S(1)}, u32[]{:S(2)}, u32[]{:S(2)}) %all-to-all-start) | async-done | bytes 1769504 | tf_op jit(solution)/shard_map/all_to_all | solution.py:208
  283.6 11.3 while.27
  299.4 56.5 %copy.113 = bf16[1,4,73728]{1,0,2:T(2,128)(2,1)} copy(bf16[1,4,73728]{2,1,0:T(4,128)(2,1)S(1)} %reshape_reshape.6) | data formatting | bytes 1179648 | tf_op jit(solution)/shard_map/reshape;reshape | solution.py:215
  356.5 400.0 %reduce.40 = bf16[73728,4]{1,0:T(8,128)(2,1)} reduce(bf16[73728,1,4]{2,1,0:T(2,128)(2,1)} %bitcast.242, bf16[]{:T(256)} %broadcast.232), dimensions={1}, to_apply=%bitcast.165.reduce_sub_computation | reduce | bytes 1179650
  756.5 51.0 %reshape.503 = bf16[4,2,36864]{2,1,0:T(2,128)(2,1)} reshape(bf16[73728,4]{1,0:T(8,128)(2,1)} %reduce.40) | data formatting | bytes 1179648
  807.5 4.6 all-to-all-start.1
  813.4 8.2 all-to-all-done.1
  821.7 61.7 %reshape.504 = bf16[73728,1,4]{2,1,0:T(2,128)(2,1)} reshape(bf16[4,2,36864]{2,1,0:T(2,128)(2,1)} %all-to-all-done.1) | data formatting | bytes 1179648
  883.4 69.2 %copy.114 = bf16[1,4,73728]{2,1,0:T(4,128)(2,1)} copy(bf16[1,4,73728]{1,0,2:T(2,128)(2,1)} %bitcast.243) | data formatting | bytes 1179648 | tf_op jit(solution)/shard_map/all_to_all | solution.py:214
  969.2 9.9 convolution_add_fusion
  979.1 8.2 convert_reduce_fusion.1
  987.3 9.1 fusion.92
  996.5 8.1 fusion.95
  1004.6 9.3 fusion.67
  1023.3 5.3 reshape.493
  1028.7 6.0 reduce.41
  1037.0 4.6 all-to-all-start.2
  1041.6 19.7 reshape.451
  1061.3 15.1 constant_dynamic-update-slice_fusion.7
  1089.0 5.5 bitcast_reduce_fusion
  1105.1 38.5 %while.28 = (s32[]{:T(128)}, f32[1,4,1024,72]{2,3,1,0:T(8,128)}, f32[1,4,1024,72]{2,3,1,0:T(8,128)S(1)}, bf16[2,1,4,512,72]{3,4,2,1,0:T(8,128)(2,1)}, bf16[2,1,4...) while((s32[]{:T(128)}, f32[1,4,1024,72]{2,3,1,0:T(8,128)}, ...), condition=%wide.region_13.14_spmd.clone, body=%wide.region_11.13_spmd.clone.sunk | while | flops 1536735232 | bytes 133357912 | solution.py:149
  1117.3 4.6 fusion.153
  1136.6 4.6 fusion.153
  1159.2 70.1 %copy.128 = bf16[3,1,4,73728]{2,0,1,3:T(4,128)(2,1)} copy(bf16[3,1,4,73728]{3,2,1,0:T(4,128)(2,1)S(1)} %pad_maximum_fusion) | data formatting | bytes 3538944 | tf_op jit(solution)/shard_map/stack | solution.py:287
  1229.2 89.9 %reshape.507 = bf16[4,2,110592]{2,1,0:T(2,128)(2,1)} reshape(bf16[73728,1,3,4]{3,2,1,0:T(4,128)(2,1)} %bitcast.169) | data formatting | bytes 3538944
  1322.9 13.6 fusion.77
  1336.6 19.7 reshape.453
  1357.8 57.9 %dynamic-update-slice.6 = f32[16,663912]{1,0:T(8,128)} dynamic-update-slice(f32[16,663912]{1,0:T(8,128)} %dynamic-update-slice.5, f32[16,331776]{1,0:T(8,128)} %reshape.453, s32[]{} %constant.143, s32[]{} %constant.145) | dynamic-update-slice | bytes 42467332
  1417.2 56.3 %reshape.455 = f32[10622592]{0:T(1024)} reshape(f32[16,663912]{1,0:T(8,128)} %dynamic-update-slice.7) | data formatting | bytes 84980736 | tf_op jit(solution)/shard_map/reshape | solution.py:54
  1473.5 102.3 %reshape.508 = bf16[73728,1,3,4]{3,2,1,0:T(4,128)(2,1)} reshape(bf16[4,2,110592]{2,1,0:T(2,128)(2,1)S(1)} %all-to-all-done.3) | data formatting | bytes 3538944
  1575.8 101.6 %copy.134 = bf16[3,1,4,4,18432]{4,3,2,0,1:T(4,128)(2,1)} copy(bf16[3,1,4,4,18432]{2,0,4,3,1:T(4,128)(2,1)} %bitcast.33) | data formatting | bytes 3538944 | tf_op jit(solution)/shard_map/all_to_all | solution.py:289
  1680.2 8.4 reshape.439
  1694.6 8.2 fusion.89
  1702.7 6.2 fusion.64
  1710.2 15.0 reshape.445
  1725.1 11.0 constant_dynamic-update-slice_fusion.6
  1737.6 16.0 dynamic-update-slice.10
  1755.2 26.6 reshape.448
  1781.8 1341.9 %all-reduce.16 = (bf16[5311872]{0:T(1024)(128)(2,1)}, bf16[10622592]{0:T(1024)(128)(2,1)}) all-reduce(f32[5311872]{0:T(1024)} %reshape.448, f32[10622592]{0:T(1024)} %reshape.455), channel_id=2, replica_groups=mesh['rep'=2,'fsdp'=4,'seq'=4] {'fsdp','seq'}, use_global_device_ids=true, to_apply=%region_26.27.clone | all-reduce | flops 15934464 | bytes 95606784
  3132.6 22.9 psum.29
  3155.6 31.3 all-gather.1
  3187.2 18.8 all-gather.2
  (284 shorter events, 193.8 us)
Async XLA Ops:
  7.2 35.2 %copy-start = (bf16[72,6912]{1,0:T(8,128)(2,1)S(1)}, bf16[72,6912]{1,0:T(8,128)(2,1)}, u32[]{:S(2)}) copy-start(bf16[72,6912]{1,0:T(8,128)(2,1)} %param.19) | copy-start | bytes 2985988
  7.2 39.2 %copy-start.51 = (u32[32]{0:T(128)S(1)}, u32[32]{0:T(128)}, u32[]{:S(2)}) copy-start(u32[32]{0:T(128)} %constant.104) | copy-start | bytes 388
  7.2 41.8 %copy-start.53 = (bf16[72]{0:T(256)(128)(2,1)S(1)}, bf16[72]{0:T(256)(128)(2,1)}, u32[]{:S(2)}) copy-start(bf16[72]{0:T(256)(128)(2,1)} %param.24) | copy-start | bytes 436
  7.2 42.0 %copy-start.54 = (bf16[72]{0:T(256)(128)(2,1)S(1)}, bf16[72]{0:T(256)(128)(2,1)}, u32[]{:S(2)}) copy-start(bf16[72]{0:T(256)(128)(2,1)} %param.28) | copy-start | bytes 436
  7.2 42.3 %copy-start.55 = (bf16[144]{0:T(256)(128)(2,1)S(1)}, bf16[144]{0:T(256)(128)(2,1)}, u32[]{:S(2)}) copy-start(bf16[144]{0:T(256)(128)(2,1)} %param.22) | copy-start | bytes 868
  7.2 42.5 %copy-start.52 = (bf16[288]{0:T(512)(128)(2,1)S(1)}, bf16[288]{0:T(512)(128)(2,1)}, u32[]{:S(2)}) copy-start(bf16[288]{0:T(512)(128)(2,1)} %param.26) | copy-start | bytes 1732
  7.2 100.5 %copy-start.10 = (bf16[1,256,1152]{2,1,0:T(8,128)(2,1)S(1)}, bf16[1,256,1152]{2,1,0:T(8,128)(2,1)}, u32[]{:S(2)}) copy-start(bf16[1,256,1152]{2,1,0:T(8,128)(2,1)} %param.17) | copy-start | bytes 1769476
  7.3 126.1 %all-reduce.13.cloned.1.call-start = ((), (), s32[]{:S(2)}) async-start(), calls=%async_computation.4 | async-start | bytes 442368 | tf_op jit(solution)/shard_map/psum | solution.py:179
  43.8 164.9 %all-gather.8.cloned.1.call-start = ((), (), s32[]{:S(2)}) async-start(), calls=%async_computation.5 | async-start | bytes 8460288 | tf_op jit(solution)/shard_map/all_gather | solution.py:185
  44.5 919.2 %all-gather.10.cloned.1.call-start = ((), (), s32[]{:S(2)}) async-start(), calls=%async_computation.6 | async-start | bytes 2820096 | tf_op jit(solution)/shard_map/all_gather | solution.py:187
  45.2 923.9 %all-gather.12.cloned.1.call-start = ((), (), s32[]{:S(2)}) async-start(), calls=%async_computation.7 | async-start | bytes 11280384 | tf_op jit(solution)/shard_map/all_gather | solution.py:189
  45.8 933.3 %all-gather.14.cloned.1.call-start = ((), (), s32[]{:S(2)}) async-start(), calls=%async_computation.8 | async-start | bytes 11280384 | tf_op jit(solution)/shard_map/all_gather | solution.py:191
  108.0 100.7 %copy-start.38 = (f32[256]{0:T(256)}, f32[256]{0:T(256)S(1)}, u32[]{:S(2)}) copy-start(f32[256]{0:T(256)S(1)} %broadcast_multiply_fusion.5) | copy-start | bytes 3076
  108.3 100.4 %copy-start.42 = (f32[256]{0:T(256)}, f32[256]{0:T(256)S(1)}, u32[]{:S(2)}) copy-start(f32[256]{0:T(256)S(1)} %add_rsqrt_fusion.1) | copy-start | bytes 3076
  134.9 73.7 %copy-start.27 = (f32[1152]{0:T(1024)}, f32[1152]{0:T(1024)S(1)}, u32[]{:S(2)}) copy-start(f32[1152]{0:T(1024)S(1)} %get-tuple-element.202) | copy-start | bytes 13828
  134.9 73.7 %copy-start.30 = (f32[1152]{0:T(1024)}, f32[1152]{0:T(1024)S(1)}, u32[]{:S(2)}) copy-start(f32[1152]{0:T(1024)S(1)} %get-tuple-element.201) | copy-start | bytes 13828
  229.4 39.6 %all-to-all-start = ((bf16[3,1,16,18432]{3,0,1,2:T(4,128)(2,1)}), bf16[3,1,16,18432]{3,0,1,2:T(4,128)(2,1)S(1)}, u32[]{:S(2)}, u32[]{:S(2)}) async-start(bf16[3,1,16,18432]{3,0,1,2:T(4,128)(2,1)} %reshape.492), calls=%async_computation | async-start | bytes 4718592 | tf_op jit(solution)/shard_map/all_to_all | solution.py:208
  278.0 5.6 copy-start.26
  294.9 61.0 %copy-start.4 = (bf16[1,4,1024,72]{2,3,1,0:T(8,128)(2,1)}, bf16[1,4,1024,72]{2,3,1,0:T(8,128)(2,1)S(1)}, u32[]{:S(2)}) copy-start(bf16[1,4,1024,72]{2,3,1,0:T(8,128)(2,1)S(1)} %get-tuple-element.443) | copy-start | bytes 1769476
  294.9 61.0 %copy-start.33 = (f32[2,1,4,512]{3,2,1,0:T(4,128)}, f32[2,1,4,512]{3,2,1,0:T(4,128)S(1)}, u32[]{:S(2)}) copy-start(f32[2,1,4,512]{3,2,1,0:T(4,128)S(1)} %get-tuple-element.405) | copy-start | bytes 49156
  807.5 14.2 all-to-all-start.1
  963.7 5.5 copy-start.29
  963.7 5.5 copy-start.32
  969.2 9.9 copy-start.36
  979.1 8.2 copy-start.9
  996.5 8.1 copy-start.14
  996.5 8.1 copy-start.18
  1037.0 48.5 %all-to-all-start.2 = ((bf16[4,2,36864]{2,1,0:T(2,128)(2,1)}), bf16[4,2,36864]{2,1,0:T(2,128)(2,1)}, u32[]{:S(2)}, u32[]{:S(2)}) async-start(bf16[4,2,36864]{2,1,0:T(2,128)(2,1)} %reshape.505), calls=%async_computation.2 | async-start | bytes 1179648 | tf_op jit(solution)/shard_map/all_to_all | solution.py:282
  1061.3 15.1 copy-start.12
  1061.3 15.1 copy-start.21
  1096.6 8.6 copy-start.34
  1113.1 4.2 copy-start.7
  1117.3 4.6 copy-start.2
  1117.3 4.8 copy-start.24
  1132.1 4.5 copy-start.7
  1136.6 4.6 copy-start.2
  1136.6 4.8 copy-start.24
  1143.6 5.1 copy-start.3
  1149.5 6.9 copy-start.22
  1319.1 154.4 %all-to-all-start.3 = ((bf16[4,2,110592]{2,1,0:T(2,128)(2,1)}), bf16[4,2,110592]{2,1,0:T(2,128)(2,1)S(1)}, u32[]{:S(2)}, u32[]{:S(2)}) async-start(bf16[4,2,110592]{2,1,0:T(2,128)(2,1)} %reshape.507), calls=%async_computation.3 | async-start | bytes 3538944 | tf_op jit(solution)/shard_map/all_to_all | solution.py:289
  1322.9 1886.3 %all-reduce.15.cloned.1.call-start = ((), (), s32[]{:S(2)}) async-start(), calls=%async_computation.9 | async-start | bytes 3989504 | tf_op jit(solution)/shard_map/psum | solution.py:332
  1336.5 19.7 copy-start.40
  1336.6 19.8 copy-start.35
  1737.6 16.0 copy-start.41
  3129.3 77.6 %copy-start.47 = (bf16[8,1,72]{2,1,0:T(2,128)(2,1)S(1)}, bf16[8,1,72]{2,1,0:T(2,128)(2,1)}, u32[]{:S(2)}) copy-start(bf16[8,1,72]{2,1,0:T(2,128)(2,1)} %copy-done.46) | copy-start | bytes 3460
  3132.5 76.1 %copy-start.44 = (bf16[1,1152]{1,0:T(2,128)(2,1)S(1)}, bf16[1,1152]{1,0:T(2,128)(2,1)}, u32[]{:S(2)}) copy-start(bf16[1,1152]{1,0:T(2,128)(2,1)} %param.18) | copy-start | bytes 6916
  3132.5 76.1 %copy-start.45 = (f32[1,1152]{1,0:T(1,128)S(1)}, f32[1,1152]{1,0:T(1,128)}, u32[]{:S(2)}) copy-start(f32[1,1152]{1,0:T(1,128)} %get-tuple-element.248) | copy-start | bytes 13828
  3209.2 5.5 copy-start.13
  (25 other events, 58.0 us)
Sparse Core Ops, SparseCore 0:
  43.9 89.4 all-reduce.12
  135.5 73.1 all-gather.7
  210.8 48.3 all-gather.9
  261.4 87.6 all-gather.11
  351.2 86.8 all-gather.13
  3129.4 68.6 all-reduce.14
where the time goes:
time: 3250 us; the launch traced here: 3230 us
  blocking collectives  1510 us (46%)
  local copies, waits for them, and re-layouts  984 us (30%)
  other arithmetic  434 us (13%)
  waiting for transfers between devices  145 us (4%)
  matrix products  128 us (4%)
    unnamed x2, blocking collectives  1400 us
    unnamed x127, local copies, waits for them, and re-layouts  428 us
    unnamed x5, other arithmetic  407 us
    all_to_all x2, local copies, waits for them, and re-layouts, on_device(): lax.all_to_all(stacked, 'seq', split_axis=3, concat_axis=2, tiled=True)  104 us
    reshape x2, local copies, waits for them, and re-layouts, pack_rows(): jnp.concatenate([array.reshape(groups, -1) for array in arrays], axis=1)  82.9 us
    another operation x4, local copies, waits for them, and re-layouts, on_device(): jnp.stack([grad_queries, grad_keys, grad_vals]).astype(jnp.bfloat16)  78 us
    all_to_all x3, local copies, waits for them, and re-layouts, on_device(): lax.all_to_all(attended.reshape(latent_count, local_heads, full_len * hea...  73.9 us
    all_gather x1, waiting for transfers between devices, on_device(): lax.all_gather(w_qkv, ('fsdp', 'seq'), axis=0, tiled=True)  73.7 us
  transfers between devices with their start and end apart: 10, of which 4 were waited for; matrix products, arithmetic and copies ran while one was open for 28% of the time, Pallas kernels for 0%

commit v1 on v0

--- a/solution.py
+++ b/solution.py
@@ -286,7 +286,9 @@
     )
     stacked = jnp.stack([grad_queries, grad_keys, grad_vals]).astype(jnp.bfloat16)
     stacked = stacked.reshape(3, latent_count, local_heads, full_len * head_size)
-    grad_tokens = lax.all_to_all(stacked, "seq", split_axis=3, concat_axis=2, tiled=True)
+    cells = jnp.split(stacked, lax.axis_size("seq"), axis=3)
+    received = lax.all_to_all(jnp.stack(cells), "seq", 0, 0)
+    grad_tokens = jnp.concatenate(received, axis=2)
     grad_proj = grad_tokens.reshape(3, latent_count, head_count, local_len, head_size).transpose(
         1, 3, 0, 2, 4
     )

time: 3250 us -> 2890 us (0.89)
  local copies, waits for them, and re-layouts: 984 us -> 629 us
    unnamed x127 -> x123, local copies, waits for them, and re-layouts: 428 us -> 239 us
    all_to_all x2 -> x0, local copies, waits for them, and re-layouts: 104 us -> none  [on_device(): lax.all_to_all(stacked, 'seq', split_axis=3, concat_axis=2, tiled=True)]
    another operation x4, local copies, waits for them, and re-layouts: 78 us -> 9.38 us  [on_device(): jnp.stack([grad_queries, grad_keys, grad_vals]).astype(jnp.bfloat16)]
  transfers between devices with their start and end apart: 10 -> 10, of which waited for: 4 -> 4; matrix products, arithmetic and copies ran while one was open for 28% -> 32% of each run, Pallas kernels for 0% -> 0%
where the time goes in v1:
time: 2890 us; the launch traced here: 2880 us
  blocking collectives  1500 us (52%)
  local copies, waits for them, and re-layouts  629 us (22%)
  other arithmetic  434 us (15%)
  waiting for transfers between devices  145 us (5%)
  matrix products  128 us (4%)
    unnamed x2, blocking collectives  1400 us
    unnamed x5, other arithmetic  407 us
    unnamed x123, local copies, waits for them, and re-layouts  239 us
    reshape x2, local copies, waits for them, and re-layouts, pack_rows(): jnp.concatenate([array.reshape(groups, -1) for array in arrays], axis=1)  83.1 us
    all_to_all x3, local copies, waits for them, and re-layouts, on_device(): lax.all_to_all(attended.reshape(latent_count, local_heads, full_len * hea...  73.9 us
    all_gather x1, waiting for transfers between devices, on_device(): lax.all_gather(w_qkv, ('fsdp', 'seq'), axis=0, tiled=True)  73.7 us
    reshape x7, local copies, waits for them, and re-layouts, pack_rows(): array.reshape(groups, -1)  59.9 us
    another operation x2, local copies, waits for them, and re-layouts, on_device(): attended.reshape(latent_count, local_heads, full_len * head_size)  59.5 us
  transfers between devices with their start and end apart: 10, of which 4 were waited for; matrix products, arithmetic and copies ran while one was open for 32% of the time, Pallas kernels for 0%

profile of v1, /device:TPU:0, one launch (start us, length us, event | category | flops | bytes accessed | tf_op | source)
XLA Modules:
  0.0 2877.0 jit_solution(979329752042765566)
XLA Ops:
  8.6 32.3 %all-gather = bf16[8,1,1152]{2,1,0:T(2,128)(2,1)S(1)} all-gather(bf16[1,1,1152]{2,1,0:T(2,128)(2,1)S(1)} %get-tuple-element.232), channel_id=1, replica_groups=mesh['rep'=2,'fsdp'=4,'seq'=4] {'rep','fsdp'}, dimensions={0}, use_global_device_ids=true | all-gather | bytes 20736 | tf_op jit(solution)/shard_map/all_gather | solution.py:171
  50.0 57.8 %all-reduce.7 = (bf16[2304]{0:T(1024)(128)(2,1)S(1)}, bf16[1152]{0:T(1024)(128)(2,1)S(1)}, bf16[1152]{0:T(1024)(128)(2,1)S(1)}, bf16[4608]{0:T(1024)(128)(2,1)S(1)}) all-reduce(bf16[2304]{0:T(1024)(128)(2,1)S(1)} %dynamic-update-slice, bf16[1152]{0:T(1024)(128)(2,1)S(1)} %dynamic-update-slice.1, ...), channel_id=1, replica_groups=mesh['rep'=2,'fsdp'=4,'seq'=4] {'fsdp','seq'}, use_global_device_ids=true, to_apply=%add | all-reduce | flops 9216 | bytes 36864
  108.2 25.0 all-reduce.13.cloned.1.call-done
  134.9 73.7 %all-gather.8.cloned.1.call-done = bf16[1152,3456]{1,0:T(8,128)(2,1)} async-done(((bf16[72,3456]{1,0:T(8,128)(2,1)}), bf16[1152,3456]{1,0:T(8,128)(2,1)}) %all-gather.8.cloned.1.call-update) | async-done | bytes 7962640 | tf_op jit(solution)/shard_map/all_gather | solution.py:185
  208.6 7.2 fusion.46
  221.4 8.1 reshape.491
  233.3 35.5 %all-to-all-done = bf16[3,1,16,18432]{3,0,1,2:T(4,128)(2,1)S(1)} async-done(((bf16[3,1,16,18432]{3,0,1,2:T(4,128)(2,1)}), bf16[3,1,16,18432]{3,0,1,2:T(4,128)(2,1)S(1)}, u32[]{:S(2)}, u32[]{:S(2)}) %all-to-all-start) | async-done | bytes 1769504 | tf_op jit(solution)/shard_map/all_to_all | solution.py:208
  283.4 11.3 while.27
  299.4 56.5 %copy.92 = bf16[1,4,73728]{1,0,2:T(2,128)(2,1)} copy(bf16[1,4,73728]{2,1,0:T(4,128)(2,1)S(1)} %reshape_reshape.9) | data formatting | bytes 1179648 | tf_op jit(solution)/shard_map/reshape;reshape | solution.py:215
  356.5 400.0 %reduce.40 = bf16[73728,4]{1,0:T(8,128)(2,1)} reduce(bf16[73728,1,4]{2,1,0:T(2,128)(2,1)} %bitcast.250, bf16[]{:T(256)} %broadcast.232), dimensions={1}, to_apply=%bitcast.175.reduce_sub_computation | reduce | bytes 1179650
  756.5 51.0 %reshape.502 = bf16[4,2,36864]{2,1,0:T(2,128)(2,1)} reshape(bf16[73728,4]{1,0:T(8,128)(2,1)} %reduce.40) | data formatting | bytes 1179648
  807.5 4.4 all-to-all-start.1
  813.2 8.2 all-to-all-done.1
  821.5 61.7 %reshape.503 = bf16[73728,1,4]{2,1,0:T(2,128)(2,1)} reshape(bf16[4,2,36864]{2,1,0:T(2,128)(2,1)} %all-to-all-done.1) | data formatting | bytes 1179648
  883.2 69.2 %copy.93 = bf16[1,4,73728]{2,1,0:T(4,128)(2,1)} copy(bf16[1,4,73728]{1,0,2:T(2,128)(2,1)} %bitcast.251) | data formatting | bytes 1179648 | tf_op jit(solution)/shard_map/all_to_all | solution.py:214
  963.7 4.2 fusion.98
  969.2 9.9 convolution_add_fusion
  979.1 8.2 convert_reduce_fusion.1
  987.4 9.1 fusion.92
  996.5 8.1 fusion.95
  1004.6 9.3 fusion.67
  1023.3 5.3 reshape.492
  1028.6 6.0 reduce.41
  1037.0 4.4 all-to-all-start.2
  1041.3 19.7 reshape.450
  1061.0 15.2 constant_dynamic-update-slice_fusion.10
  1079.6 4.5 reshape.445
  1088.4 5.5 bitcast_reduce_fusion
  1104.5 38.9 %while.28 = (s32[]{:T(128)}, f32[1,4,1024,72]{2,3,1,0:T(8,128)}, f32[1,4,1024,72]{2,3,1,0:T(8,128)S(1)}, bf16[2,1,4,512,72]{3,4,2,1,0:T(8,128)(2,1)}, bf16[2,1,4...) while((s32[]{:T(128)}, f32[1,4,1024,72]{2,3,1,0:T(8,128)}, ...), condition=%wide.region_13.14_spmd.clone, body=%wide.region_11.13_spmd.clone.sunk | while | flops 1536735232 | bytes 133357912 | solution.py:149
  1112.8 4.2 fusion.152
  1117.0 4.6 fusion.153
  1131.9 4.5 fusion.152
  1136.4 4.6 fusion.153
  1172.5 13.7 fusion.77
  1186.2 19.7 reshape.452
  1207.5 57.9 %dynamic-update-slice.6 = f32[16,663912]{1,0:T(8,128)} dynamic-update-slice(f32[16,663912]{1,0:T(8,128)} %dynamic-update-slice.5, f32[16,331776]{1,0:T(8,128)} %reshape.452, s32[]{} %constant.143, s32[]{} %constant.145) | dynamic-update-slice | bytes 42467332
  1266.9 56.4 %reshape.454 = f32[10622592]{0:T(1024)} reshape(f32[16,663912]{1,0:T(8,128)} %dynamic-update-slice.7) | data formatting | bytes 84980736 | tf_op jit(solution)/shard_map/reshape | solution.py:54
  1325.3 8.8 reshape_reshape.11
  1340.0 8.2 fusion.89
  1348.2 6.2 fusion.64
  1355.6 15.2 reshape.444
  1370.8 11.0 constant_dynamic-update-slice_fusion.9
  1383.3 16.0 dynamic-update-slice.10
  1400.8 26.6 reshape.447
  1427.5 1341.9 %all-reduce.16 = (bf16[5311872]{0:T(1024)(128)(2,1)}, bf16[10622592]{0:T(1024)(128)(2,1)}) all-reduce(f32[5311872]{0:T(1024)} %reshape.447, f32[10622592]{0:T(1024)} %reshape.454), channel_id=2, replica_groups=mesh['rep'=2,'fsdp'=4,'seq'=4] {'fsdp','seq'}, use_global_device_ids=true, to_apply=%region_26.27.clone | all-reduce | flops 15934464 | bytes 95606784
  2778.3 22.9 psum.29
  2801.2 31.3 %all-gather.1 = bf16[8,1,6912]{2,1,0:T(2,128)(2,1)S(1)} all-gather(bf16[1,1,6912]{2,1,0:T(2,128)(2,1)S(1)} %bitcast.271), channel_id=1, replica_groups=mesh['rep'=2,'fsdp'=4,'seq'=4] {'rep','fsdp'}, dimensions={0}, use_global_device_ids=true | all-gather | bytes 124416 | tf_op jit(solution)/shard_map/all_gather | solution.py:315
  2832.9 18.8 all-gather.2
  (281 shorter events, 185.4 us)
Async XLA Ops:
  7.2 35.1 %copy-start = (bf16[72,6912]{1,0:T(8,128)(2,1)S(1)}, bf16[72,6912]{1,0:T(8,128)(2,1)}, u32[]{:S(2)}) copy-start(bf16[72,6912]{1,0:T(8,128)(2,1)} %param.19) | copy-start | bytes 2985988
  7.2 126.1 %all-reduce.13.cloned.1.call-start = ((), (), s32[]{:S(2)}) async-start(), calls=%async_computation.4 | async-start | bytes 442368 | tf_op jit(solution)/shard_map/psum | solution.py:179
  42.3 4.1 copy-start.49
  42.3 6.6 copy-start.51
  42.3 6.9 copy-start.52
  42.3 7.1 copy-start.53
  42.3 7.4 copy-start.50
  42.3 65.4 %copy-start.10 = (bf16[1,256,1152]{2,1,0:T(8,128)(2,1)S(1)}, bf16[1,256,1152]{2,1,0:T(8,128)(2,1)}, u32[]{:S(2)}) copy-start(bf16[1,256,1152]{2,1,0:T(8,128)(2,1)} %param.17) | copy-start | bytes 1769476
  43.7 164.9 %all-gather.8.cloned.1.call-start = ((), (), s32[]{:S(2)}) async-start(), calls=%async_computation.5 | async-start | bytes 8460288 | tf_op jit(solution)/shard_map/all_gather | solution.py:185
  44.5 919.2 %all-gather.10.cloned.1.call-start = ((), (), s32[]{:S(2)}) async-start(), calls=%async_computation.6 | async-start | bytes 2820096 | tf_op jit(solution)/shard_map/all_gather | solution.py:187
  45.2 924.0 %all-gather.12.cloned.1.call-start = ((), (), s32[]{:S(2)}) async-start(), calls=%async_computation.7 | async-start | bytes 11280384 | tf_op jit(solution)/shard_map/all_gather | solution.py:189
  45.8 933.3 %all-gather.14.cloned.1.call-start = ((), (), s32[]{:S(2)}) async-start(), calls=%async_computation.8 | async-start | bytes 11280384 | tf_op jit(solution)/shard_map/all_gather | solution.py:191
  107.9 100.7 %copy-start.36 = (f32[256]{0:T(256)}, f32[256]{0:T(256)S(1)}, u32[]{:S(2)}) copy-start(f32[256]{0:T(256)S(1)} %broadcast_multiply_fusion.5) | copy-start | bytes 3076
  108.2 100.4 %copy-start.40 = (f32[256]{0:T(256)}, f32[256]{0:T(256)S(1)}, u32[]{:S(2)}) copy-start(f32[256]{0:T(256)S(1)} %add_rsqrt_fusion.1) | copy-start | bytes 3076
  134.9 73.7 %copy-start.27 = (f32[1152]{0:T(1024)}, f32[1152]{0:T(1024)S(1)}, u32[]{:S(2)}) copy-start(f32[1152]{0:T(1024)S(1)} %get-tuple-element.187) | copy-start | bytes 13828
  134.9 73.7 %copy-start.30 = (f32[1152]{0:T(1024)}, f32[1152]{0:T(1024)S(1)}, u32[]{:S(2)}) copy-start(f32[1152]{0:T(1024)S(1)} %get-tuple-element.186) | copy-start | bytes 13828
  229.4 39.4 %all-to-all-start = ((bf16[3,1,16,18432]{3,0,1,2:T(4,128)(2,1)}), bf16[3,1,16,18432]{3,0,1,2:T(4,128)(2,1)S(1)}, u32[]{:S(2)}, u32[]{:S(2)}) async-start(bf16[3,1,16,18432]{3,0,1,2:T(4,128)(2,1)} %reshape.491), calls=%async_computation | async-start | bytes 4718592 | tf_op jit(solution)/shard_map/all_to_all | solution.py:208
  277.8 5.6 copy-start.26
  294.7 61.3 %copy-start.4 = (bf16[1,4,1024,72]{2,3,1,0:T(8,128)(2,1)}, bf16[1,4,1024,72]{2,3,1,0:T(8,128)(2,1)S(1)}, u32[]{:S(2)}) copy-start(bf16[1,4,1024,72]{2,3,1,0:T(8,128)(2,1)S(1)} %get-tuple-element.431) | copy-start | bytes 1769476
  294.7 61.3 %copy-start.33 = (f32[2,1,4,512]{3,2,1,0:T(4,128)}, f32[2,1,4,512]{3,2,1,0:T(4,128)S(1)}, u32[]{:S(2)}) copy-start(f32[2,1,4,512]{3,2,1,0:T(4,128)S(1)} %get-tuple-element.393) | copy-start | bytes 49156
  807.5 14.0 all-to-all-start.1
  963.7 5.5 copy-start.29
  963.7 5.5 copy-start.32
  969.2 9.9 copy-start.35
  979.1 8.2 copy-start.9
  996.5 8.1 copy-start.14
  996.5 8.1 copy-start.18
  1037.0 47.9 %all-to-all-start.2 = ((bf16[4,2,36864]{2,1,0:T(2,128)(2,1)}), bf16[4,2,36864]{2,1,0:T(2,128)(2,1)}, u32[]{:S(2)}, u32[]{:S(2)}) async-start(bf16[4,2,36864]{2,1,0:T(2,128)(2,1)} %reshape.504), calls=%async_computation.2 | async-start | bytes 1179648 | tf_op jit(solution)/shard_map/all_to_all | solution.py:282
  1061.0 15.2 copy-start.12
  1061.0 15.2 copy-start.21
  1098.3 6.2 copy-start.34
  1112.8 4.2 copy-start.7
  1117.0 4.6 copy-start.2
  1117.0 4.8 copy-start.24
  1131.9 4.5 copy-start.7
  1136.4 4.6 copy-start.2
  1136.4 4.8 copy-start.24
  1145.6 6.0 copy-start.3
  1157.6 3.6 copy-start.22
  1168.7 3.8 copy-start.19
  1168.7 154.6 %all-to-all-start.3 = ((bf16[4,3,1,4,18432]{4,3,1,2,0:T(4,128)(2,1)}), bf16[4,3,1,4,18432]{4,3,1,2,0:T(4,128)(2,1)S(1)}, u32[]{:S(2)}, u32[]{:S(2)}) async-start(bf16[4,3,1,4,18432]{4,3,1,2,0:T(4,128)(2,1)} %pad_maximum_fusion), calls=%async_computation.3 | async-start | bytes 3538944 | tf_op jit(solution)/shard_map/all_to_all | solution.py:290
  1172.4 1682.4 %all-reduce.15.cloned.1.call-start = ((), (), s32[]{:S(2)}) async-start(), calls=%async_computation.9 | async-start | bytes 3989504 | tf_op jit(solution)/shard_map/psum | solution.py:334
  1186.2 19.7 copy-start.38
  1383.3 16.0 copy-start.39
  2778.2 74.3 %copy-start.45 = (bf16[8,1,72]{2,1,0:T(2,128)(2,1)S(1)}, bf16[8,1,72]{2,1,0:T(2,128)(2,1)}, u32[]{:S(2)}) copy-start(bf16[8,1,72]{2,1,0:T(2,128)(2,1)} %copy-done.44) | copy-start | bytes 3460
  2832.5 21.7 copy-start.42
  2832.5 21.7 copy-start.43
  2854.9 5.5 copy-start.13
  (23 other events, 50.4 us)
Sparse Core Ops, SparseCore 0:
  43.8 89.4 all-reduce.12
  135.5 73.1 all-gather.7
  210.8 48.3 all-gather.9
  261.4 87.5 all-gather.11
  351.1 86.8 all-gather.13
  2775.1 68.6 all-reduce.14
